TPU v7x, 32 devices: a whole 2x2x4 slice. The times are simulated.
32 devices in a mesh: mode: 8 (over y, x, core), orb: 4 (over z).
Axes of the slice: x: 2, y: 2, z: 4, core: 2. Of those that a mesh axis runs over, the one named last changes fastest.
Arguments:
- correlators: float32 [512, 2, 256, 256], P('mode', None, 'orb'), may hold values from -6 to 6
- density: float32 [2, 256, 256], P(None, 'orb'), may hold values from -6 to 6
- bare_hamiltonian: float32 [2, 256, 256], P(None, 'orb'), may hold values from -0.375 to 0.375
- coupling: float32 [512], P('mode'), may hold values from -0.25 to 0.25
- propagator: float32 [512, 512], P('mode'), may hold values from -0.25 to 0.25
Outputs:
- correlators_out: float32 [512, 2, 256, 256], P('mode', None, 'orb')
- density_out: float32 [2, 256, 256], P(None, 'orb')
All inputs are finite; a program needn't handle non-finite values.
Results may differ from a plain program's by a relative error of at most 0.0001.
Values sent between devices are 32-bit elements; how exact they have to be, the bound alone decides.
No kernel may reach another device: no remote copies, remote signals or barrier semaphores. Data moves between devices by JAX's collectives and lax.ppermute only.
A program may use at most 128 MiB of HBM per device.

v0:
```python
import jax
import jax.numpy as jnp
from jax import lax
from jax.sharding import PartitionSpec as P

time_step = 0.1
field_weight = 0.0625


def contract(form, first, second):
    return jnp.einsum(form, first, second, precision=lax.Precision.HIGHEST)


def left_product(matrix, stack):
    real = contract("ij,mjk->mik", matrix[0], stack[:, 0]) - contract(
        "ij,mjk->mik", matrix[1], stack[:, 1]
    )
    imag = contract("ij,mjk->mik", matrix[0], stack[:, 1]) + contract(
        "ij,mjk->mik", matrix[1], stack[:, 0]
    )
    return jnp.stack([real, imag], axis=1)


def right_product(stack, matrix):
    real = contract("mij,jk->mik", stack[:, 0], matrix[0]) - contract(
        "mij,jk->mik", stack[:, 1], matrix[1]
    )
    imag = contract("mij,jk->mik", stack[:, 0], matrix[1]) + contract(
        "mij,jk->mik", stack[:, 1], matrix[0]
    )
    return jnp.stack([real, imag], axis=1)


def advance(stack, commut, weights, dens):
    turned = jnp.stack([commut[:, 1], -commut[:, 0]], axis=1)
    return stack + time_step * turned + time_step * weights[:, None, None, None] * dens[None]


def modes_substep(stacks, dens, hamil, bare_full, weights):
    commut = left_product(hamil, stacks) - right_product(stacks, hamil)
    updated = advance(stacks, commut, weights, dens)
    partial_value = contract("m,mcij->cij", weights, updated)
    collision = lax.psum(partial_value, ("mode", "orb"))
    dens = dens + time_step * collision
    return (updated, dens, bare_full + field_weight * dens)


def to_whole(stacks):
    return lax.all_to_all(stacks, "orb", split_axis=0, concat_axis=2, tiled=True)


def to_split(stacks):
    return lax.all_to_all(stacks, "orb", split_axis=2, concat_axis=0, tiled=True)


def propagate(stacks, propagator):
    local_modes = stacks.shape[0]
    groups = lax.axis_size("mode")
    flat = stacks.reshape(local_modes, groups, -1)
    spread = lax.all_to_all(flat, "mode", split_axis=1, concat_axis=0, tiled=True)
    entries = spread[:, 0, :]
    mixed = contract("mn,nx->mx", lax.all_gather(propagator, "mode", axis=0, tiled=True), entries)
    returned = lax.all_to_all(mixed[:, None, :], "mode", split_axis=0, concat_axis=1, tiled=True)
    return returned.reshape(stacks.shape)


def on_device(correlators, density, bare_hamiltonian, coupling, propagator):
    dens, bare_full = (
        lax.all_gather(density, "orb", axis=1, tiled=True),
        lax.all_gather(bare_hamiltonian, "orb", axis=1, tiled=True),
    )
    hamil = bare_full + field_weight * dens
    owned = correlators.shape[0] // lax.axis_size("orb")
    weights = lax.dynamic_slice_in_dim(coupling, lax.axis_index("orb") * owned, owned, 0)
    whole = to_whole(correlators)
    for turn in range(2):
        whole, dens, hamil = modes_substep(whole, dens, hamil, bare_full, weights)
    stacks = propagate(to_split(whole), propagator)
    whole = to_whole(stacks)
    whole, dens, hamil = modes_substep(whole, dens, hamil, bare_full, weights)
    stacks = to_split(whole)
    row_count = density.shape[1]
    dens_rows = lax.dynamic_slice_in_dim(dens, lax.axis_index("orb") * row_count, row_count, 1)
    return (stacks, dens_rows)


def solution(mesh):
    in_specs = (
        P("mode", None, "orb", None),
        P(None, "orb", None),
        P(None, "orb", None),
        P("mode"),
        P("mode", None),
    )
    out_specs = (P("mode", None, "orb", None), P(None, "orb", None))
    return jax.shard_map(
        on_device, mesh=mesh, in_specs=in_specs, out_specs=out_specs, check_vma=False
    )
```

profile of v0, /device:TPU:0, one launch (start us, length us, event | category | flops | bytes accessed | tf_op | source)
XLA Modules:
  0.0 1640.5 jit_solution(9633585185455088017)
XLA Ops:
  8.0 6.5 all-to-all-start
  14.6 194.0 %all_gather.10 = f32[2,256,256]{2,1,0:T(8,128)S(1)} all-gather(f32[2,64,256]{2,1,0:T(8,128)S(1)} %copy-done.12), channel_id=1, replica_groups=mesh['mode'=8,'orb'=4] {'orb'}, dimensions={1}, use_global_device_ids=true | all-gather | bytes 655360 | tf_op jit(solution)/shard_map/all_gather | solution.py:69
  208.6 15.9 all_gather.9
  224.6 4.1 copy.64
  235.6 3.8 fusion.15
  239.4 4.1 fusion.14
  250.7 13.2 subtract_bitcast_fusion.5
  263.9 5.2 add_bitcast_fusion.5
  274.6 4.9 fusion.1
  282.9 7.8 fusion.10
  291.5 130.2 %all-reduce.4.cloned.1.call-done = f32[2,256,256]{2,1,0:T(8,128)} async-done(((f32[2,256,256]{2,1,0:T(8,128)}), f32[2,256,256]{2,1,0:T(8,128)}) %all-reduce.4.cloned.1.call-update) | async-done | bytes 524304 | tf_op jit(solution)/shard_map/psum | solution.py:43
  423.8 6.1 fusion.21
  433.4 4.0 fusion.23
  437.4 4.0 fusion.22
  441.4 4.3 subtract_bitcast_fusion.2
  445.8 5.0 add_bitcast_fusion.2
  450.7 5.5 subtract_bitcast_fusion.3
  456.3 5.4 add_bitcast_fusion.3
  461.7 4.3 maximum_subtract_fusion.1
  466.0 4.3 fusion.40
  470.3 6.9 fusion.3
  477.2 8.3 copy.81
  485.4 186.8 %all_to_all.99 = f32[16,2,256,256]{3,0,1,2:T(8,128)S(1)} all-to-all(f32[16,2,256,256]{3,0,1,2:T(8,128)} %copy.81), channel_id=1, replica_groups=mesh['mode'=8,'orb'=4] {'orb'}, dimensions={2} | all-to-all | bytes 16777216 | tf_op jit(solution)/shard_map/all_to_all | solution.py:53
  672.3 8.3 copy.145
  680.5 9.4 reshape.18
  689.9 11.6 copy.83
  701.5 5.0 all-to-all-start.2
  707.1 56.9 %all-gather.2.cloned.1.call-done = f32[512,512]{1,0:T(8,128)} async-done(((f32[64,512]{1,0:T(8,128)}), f32[512,512]{1,0:T(8,128)}) %all-gather.2.cloned.1.call-update) | async-done | bytes 1048592 | tf_op jit(solution)/shard_map/all_gather | solution.py:62
  764.0 40.7 %all-to-all-done.2 = f32[64,8,4096]{2,0,1:T(8,128)} async-done(((f32[64,8,4096]{2,0,1:T(8,128)}), f32[64,8,4096]{2,0,1:T(8,128)}, u32[]{:S(2)}, u32[]{:S(2)}) %all-to-all-start.2) | async-done | bytes 8388640 | tf_op jit(solution)/shard_map/all_to_all | solution.py:60
  804.7 30.3 %convolution_bitcast_fusion = f32[512,1,4096]{0,2,1:T(8,128)} fusion(f32[512,4096]{1,0:T(8,128)} %bitcast.41, f32[512,512]{1,0:T(8,128)} %all-gather.2.cloned.1.call-done), kind=kOutput, calls=%fused_computation.19 | convolution fusion | flops 12884901888 | bytes 17825792 | tf_op jit(solution)/shard_map/mn,nx->mx/dot_general | solution.py:11
  835.0 19.3 %copy.84 = f32[512,1,4096]{2,1,0:T(1,128)} copy(f32[512,1,4096]{0,2,1:T(8,128)} %convolution_bitcast_fusion) | data formatting | bytes 16777216 | tf_op jit(solution)/shard_map/broadcast_in_dim | solution.py:63
  854.3 97.8 %all_to_all.100 = f32[512,1,4096]{2,1,0:T(1,128)S(1)} all-to-all(f32[512,1,4096]{2,1,0:T(1,128)} %copy.84), channel_id=1, replica_groups=mesh['mode'=8,'orb'=4] {'mode'}, dimensions={0} | all-to-all | bytes 16777216 | tf_op jit(solution)/shard_map/all_to_all | solution.py:63
  952.1 8.1 copy.134
  960.2 8.5 copy.85
  968.6 9.4 reshape.19
  978.0 5.7 all-to-all-start.4
  983.8 12.9 fusion.8
  997.5 272.8 %all-reduce.6.cloned.1.call-done = f32[2,256,256]{2,1,0:T(8,128)} async-done(((f32[2,256,256]{2,1,0:T(8,128)}), f32[2,256,256]{2,1,0:T(8,128)}) %all-reduce.6.cloned.1.call-update) | async-done | bytes 524304 | tf_op jit(solution)/shard_map/psum | solution.py:43
  1271.5 4.0 copy.86
  1282.4 4.2 fusion.31
  1286.6 4.0 fusion.30
  1297.7 4.3 subtract_bitcast_fusion.1
  1302.0 5.5 add_bitcast_fusion.1
  1319.6 8.3 copy.95
  1327.9 5.6 all-to-all-start.5
  1333.6 12.7 fusion.6
  1347.1 272.6 %all-reduce.8.cloned.1.call-done = f32[2,256,256]{2,1,0:T(8,128)} async-done(((f32[2,256,256]{2,1,0:T(8,128)}), f32[2,256,256]{2,1,0:T(8,128)}) %all-reduce.8.cloned.1.call-update) | async-done | bytes 524304 | tf_op jit(solution)/shard_map/psum | solution.py:43
  1621.3 11.6 copy.96
  (68 shorter events, 60.6 us)
Async XLA Ops:
  8.0 6.5 copy-start.14
  8.0 6.6 copy-start.12
  8.0 200.5 %copy-start.13 = (f32[2,64,256]{2,1,0:T(8,128)S(1)}, f32[2,64,256]{2,1,0:T(8,128)}, u32[]{:S(2)}) copy-start(f32[2,64,256]{2,1,0:T(8,128)} %param.7) | copy-start | bytes 393220
  8.0 216.6 %all-to-all-start = ((f32[64,2,64,256]{3,2,1,0:T(8,128)}), f32[64,2,64,256]{3,2,1,0:T(8,128)}, u32[]{:S(2)}, u32[]{:S(2)}) async-start(f32[64,2,64,256]{3,2,1,0:T(8,128)} %param.5), calls=%async_computation | async-start | bytes 16777216 | tf_op jit(solution)/shard_map/all_to_all | solution.py:49
  14.5 407.2 %all-reduce.4.cloned.1.call-start = ((), (), s32[]{:S(2)}) async-start(), calls=%async_computation.6 | async-start | bytes 1048576 | tf_op jit(solution)/shard_map/psum | solution.py:43
  208.6 213.2 %copy-start.8 = (f32[2,256,256]{2,1,0:T(8,128)}, f32[2,256,256]{2,1,0:T(8,128)S(1)}, u32[]{:S(2)}) copy-start(f32[2,256,256]{2,1,0:T(8,128)S(1)} %all_gather.10) | copy-start | bytes 1572868
  224.5 197.2 %copy-start.9 = (f32[2,256,256]{2,1,0:T(8,128)}, f32[2,256,256]{2,1,0:T(8,128)S(1)}, u32[]{:S(2)}) copy-start(f32[2,256,256]{2,1,0:T(8,128)S(1)} %all_gather.9) | copy-start | bytes 1572868
  228.7 45.9 %copy-start = (f32[4,16,2,64,256]{4,3,0,1,2:T(8,128)}, f32[4,16,2,64,256]{4,3,0,1,2:T(8,128)S(1)}, u32[]{:S(2)}) copy-start(f32[4,16,2,64,256]{4,3,0,1,2:T(8,128)S(1)} %copy.64) | copy-start | bytes 25165828
  274.6 4.9 copy-start.5
  279.5 3.4 copy-start.1
  421.7 8.2 copy-start.2
  456.3 5.4 copy-start.7
  456.3 14.0 slice-start
  461.7 8.6 slice-start.1
  466.0 4.3 copy-start.6
  477.2 8.3 copy-start.3
  701.5 103.2 %all-to-all-start.2 = ((f32[64,8,4096]{2,0,1:T(8,128)}), f32[64,8,4096]{2,0,1:T(8,128)}, u32[]{:S(2)}, u32[]{:S(2)}) async-start(f32[64,8,4096]{2,0,1:T(8,128)} %copy.83), calls=%async_computation.2 | async-start | bytes 16777216 | tf_op jit(solution)/shard_map/all_to_all | solution.py:60
  706.5 57.5 %all-gather.2.cloned.1.call-start = ((), (), s32[]{:S(2)}) async-start(), calls=%async_computation.7 | async-start | bytes 1179648 | tf_op jit(solution)/shard_map/all_gather | solution.py:62
  978.0 293.5 %all-to-all-start.4 = ((f32[64,2,64,256]{3,2,1,0:T(8,128)}), f32[64,2,64,256]{3,2,1,0:T(8,128)}, u32[]{:S(2)}, u32[]{:S(2)}) async-start(f32[64,2,64,256]{3,2,1,0:T(8,128)} %reshape.19), calls=%async_computation.4 | async-start | bytes 16777216 | tf_op jit(solution)/shard_map/all_to_all | solution.py:49
  983.7 286.7 %copy-start.10 = (f32[2,256,256]{2,1,0:T(8,128)S(1)}, f32[2,256,256]{2,1,0:T(8,128)}, u32[]{:S(2)}) copy-start(f32[2,256,256]{2,1,0:T(8,128)} %copy-done.9) | copy-start | bytes 1572868
  983.7 286.7 %copy-start.11 = (f32[2,256,256]{2,1,0:T(8,128)S(1)}, f32[2,256,256]{2,1,0:T(8,128)}, u32[]{:S(2)}) copy-start(f32[2,256,256]{2,1,0:T(8,128)} %get-tuple-element.5) | copy-start | bytes 1572868
  983.7 286.7 %all-reduce.6.cloned.1.call-start = ((), (), s32[]{:S(2)}) async-start(), calls=%async_computation.8 | async-start | bytes 1048576 | tf_op jit(solution)/shard_map/psum | solution.py:43
  1316.4 3.3 copy-start.4
  1327.9 293.5 %all-to-all-start.5 = ((f32[16,2,256,256]{3,0,1,2:T(8,128)}), f32[16,2,256,256]{3,0,1,2:T(8,128)}, u32[]{:S(2)}, u32[]{:S(2)}) async-start(f32[16,2,256,256]{3,0,1,2:T(8,128)} %copy.95), calls=%async_computation.5 | async-start | bytes 16777216 | tf_op jit(solution)/shard_map/all_to_all | solution.py:53
  1333.5 286.2 %all-reduce.8.cloned.1.call-start = ((), (), s32[]{:S(2)}) async-start(), calls=%async_computation.9 | async-start | bytes 1048576 | tf_op jit(solution)/shard_map/psum | solution.py:43
Sparse Core Ops, SparseCore 0:
  291.7 130.0 all-reduce.3
  997.6 272.6 all-reduce.5
  1347.2 272.4 all-reduce.7
Sparse Core Ops, SparseCore 1:
  708.9 55.1 all-gather.1
where the time goes:
time: 1650 us; the launch traced here: 1640 us
  waiting for transfers between devices  774 us (47%)
  blocking collectives  494 us (30%)
  matrix products  174 us (11%)
  local copies, waits for them, and re-layouts  120 us (7%)
  other arithmetic  39.6 us (2%)
  starting transfers between devices  22.9 us (1%)
    psum x3, waiting for transfers between devices, modes_substep(): collision = lax.psum(partial_value, ('mode', 'orb'))  676 us
    all_gather x1, blocking collectives, on_device(): lax.all_gather(density, 'orb', axis=1, tiled=True)  194 us
    all_to_all x1, blocking collectives, to_split(): lax.all_to_all(stacks, 'orb', split_axis=2, concat_axis=0, tiled=True)  187 us
    dot_general x28, matrix products, contract(): return jnp.einsum(form, first, second, precision=lax.Precision.HIGHEST)  174 us
    all_to_all x1, blocking collectives, propagate(): lax.all_to_all(mixed[:, None, :], 'mode', split_axis=0, concat_axis=1, ti...  97.8 us
    all_gather x1, waiting for transfers between devices, propagate(): lax.all_gather(propagator, 'mode', axis=0, tiled=True)  56.9 us
    all_to_all x1, waiting for transfers between devices, propagate(): lax.all_to_all(flat, 'mode', split_axis=1, concat_axis=0, tiled=True)  40.7 us
  transfers between devices with their start and end apart: 8, of which 5 were waited for; matrix products, arithmetic and copies ran while one was open for 2% of the time, Pallas kernels for 0%

commit v1 on v0

--- a/solution.py
+++ b/solution.py
@@ -40,7 +40,8 @@
     commut = left_product(hamil, stacks) - right_product(stacks, hamil)
     updated = advance(stacks, commut, weights, dens)
     partial_value = contract("m,mcij->cij", weights, updated)
-    collision = lax.psum(partial_value, ("mode", "orb"))
+    parts = lax.all_gather(partial_value, ("mode", "orb"), axis=0, tiled=False)
+    collision = parts.sum(axis=0)
     dens = dens + time_step * collision
     return (updated, dens, bare_full + field_weight * dens)
 

time: 1650 us -> 1610 us (0.976)
  blocking collectives: 494 us -> 308 us
  waiting for transfers between devices: 774 us -> 884 us
  other arithmetic: 39.6 us -> 57.1 us
    psum x3 -> x0, waiting for transfers between devices: 676 us -> none  [modes_substep(): collision = lax.psum(partial_value, ('mode', 'orb'))]
    all_to_all x1 -> x2, waiting for transfers between devices: 0.01 us -> 498 us  [to_split(): lax.all_to_all(stacks, 'orb', split_axis=2, concat_axis=0, tiled=True)]
    all_to_all x1 -> x0, blocking collectives: 187 us -> none  [to_split(): lax.all_to_all(stacks, 'orb', split_axis=2, concat_axis=0, tiled=True)]
    all_to_all x2, waiting for transfers between devices: 0.01 us -> 176 us  [to_whole(): lax.all_to_all(stacks, 'orb', split_axis=0, concat_axis=2, tiled=True)]
    all_gather x0 -> x3, waiting for transfers between devices: none -> 116 us  [modes_substep(): parts = lax.all_gather(partial_value, ('mode', 'orb'), axis=0, tiled=False)]
    all_gather x1, waiting for transfers between devices: 56.9 us -> 0.03 us  [propagate(): lax.all_gather(propagator, 'mode', axis=0, tiled=True)]
    all_to_all x1, waiting for transfers between devices: 40.7 us -> 94 us  [propagate(): lax.all_to_all(flat, 'mode', split_axis=1, concat_axis=0, tiled=True)]
    reduce_sum x0 -> x3, other arithmetic: none -> 20.8 us  [modes_substep(): collision = parts.sum(axis=0)]
  transfers between devices with their start and end apart: 8 -> 9, of which waited for: 5 -> 5; matrix products, arithmetic and copies ran while one was open for 2% -> 10% of each run, Pallas kernels for 0% -> 0%
where the time goes in v1:
time: 1610 us; the launch traced here: 1590 us
  waiting for transfers between devices  884 us (55%)
  blocking collectives  308 us (19%)
  matrix products  170 us (11%)
  local copies, waits for them, and re-layouts  131 us (8%)
  other arithmetic  57.1 us (4%)
  starting transfers between devices  28.5 us (2%)
  between operations  16.4 us (1%)
    all_to_all x2, waiting for transfers between devices, to_split(): lax.all_to_all(stacks, 'orb', split_axis=2, concat_axis=0, tiled=True)  498 us
    all_gather x1, blocking collectives, on_device(): lax.all_gather(density, 'orb', axis=1, tiled=True)  194 us
    all_to_all x2, waiting for transfers between devices, to_whole(): lax.all_to_all(stacks, 'orb', split_axis=0, concat_axis=2, tiled=True)  176 us
    dot_general x28, matrix products, contract(): return jnp.einsum(form, first, second, precision=lax.Precision.HIGHEST)  170 us
    all_gather x3, waiting for transfers between devices, modes_substep(): parts = lax.all_gather(partial_value, ('mode', 'orb'), axis=0, tiled=False)  116 us
    all_to_all x1, blocking collectives, propagate(): lax.all_to_all(mixed[:, None, :], 'mode', split_axis=0, concat_axis=1, ti...  97.8 us
    all_to_all x1, waiting for transfers between devices, propagate(): lax.all_to_all(flat, 'mode', split_axis=1, concat_axis=0, tiled=True)  94 us
  transfers between devices with their start and end apart: 9, of which 5 were waited for; matrix products, arithmetic and copies ran while one was open for 10% of the time, Pallas kernels for 0%

profile of v1, /device:TPU:0, one launch (start us, length us, event | category | flops | bytes accessed | tf_op | source)
XLA Modules:
  0.0 1594.7 jit_solution(8836876320927381221)
XLA Ops:
  8.0 6.5 all-to-all-start
  14.6 194.0 %all_gather.28 = f32[2,256,256]{2,1,0:T(8,128)S(1)} all-gather(f32[2,64,256]{2,1,0:T(8,128)S(1)} %copy-done.11), channel_id=1, replica_groups=mesh['mode'=8,'orb'=4] {'orb'}, dimensions={1}, use_global_device_ids=true | all-gather | bytes 655360 | tf_op jit(solution)/shard_map/all_gather | solution.py:70
  208.6 15.9 all_gather.27
  224.6 4.1 copy.64
  239.5 4.1 fusion.14
  254.6 14.8 add_bitcast_fusion.5
  274.9 4.9 fusion.1
  283.2 7.8 fusion.10
  291.9 115.6 %all-gather.10.cloned.1.call-done = f32[64,256,256]{2,1,0:T(8,128)} async-done(((f32[2,256,256]{2,1,0:T(8,128)}), f32[64,256,256]{2,1,0:T(8,128)}) %all-gather.10.cloned.1.call-update) | async-done | bytes 16777232 | tf_op jit(solution)/shard_map/all_gather | solution.py:43
  407.5 6.9 reduce_sum.27
  415.3 5.4 fusion.21
  420.7 5.7 fusion.20
  426.4 4.0 fusion.23
  430.4 4.0 fusion.22
  438.3 5.2 add_bitcast_fusion.2
  443.5 5.5 subtract_bitcast_fusion.3
  449.0 5.4 add_bitcast_fusion.3
  454.5 4.3 maximum_subtract_fusion.1
  458.8 4.3 fusion.40
  463.1 6.7 fusion.3
  473.1 8.3 copy.81
  481.3 5.7 all-to-all-start.1
  487.6 12.8 fusion.8
  501.3 245.2 %all-to-all-done.1 = f32[16,2,256,256]{3,0,1,2:T(8,128)} async-done(((f32[16,2,256,256]{3,0,1,2:T(8,128)}), f32[16,2,256,256]{3,0,1,2:T(8,128)}, u32[]{:S(2)}, u32[]{:S(2)}) %all-to-all-start.1) | async-done | bytes 8388640 | tf_op jit(solution)/shard_map/all_to_all | solution.py:54
  746.5 12.2 copy.145
  758.7 9.6 reshape.18
  768.4 11.6 copy.83
  780.0 5.0 all-to-all-start.2
  785.0 94.0 %all-to-all-done.2 = f32[64,8,4096]{2,0,1:T(8,128)} async-done(((f32[64,8,4096]{2,0,1:T(8,128)}), f32[64,8,4096]{2,0,1:T(8,128)}, u32[]{:S(2)}, u32[]{:S(2)}) %all-to-all-start.2) | async-done | bytes 8388640 | tf_op jit(solution)/shard_map/all_to_all | solution.py:61
  879.0 29.9 %convolution_bitcast_fusion = f32[512,1,4096]{0,2,1:T(8,128)} fusion(f32[512,4096]{1,0:T(8,128)} %bitcast.42, f32[512,512]{1,0:T(8,128)} %all-gather.8.cloned.1.call-done), kind=kOutput, calls=%fused_computation.19 | convolution fusion | flops 12884901888 | bytes 17825792 | tf_op jit(solution)/shard_map/mn,nx->mx/dot_general | solution.py:11
  908.9 19.3 %copy.84 = f32[512,1,4096]{2,1,0:T(1,128)} copy(f32[512,1,4096]{0,2,1:T(8,128)} %convolution_bitcast_fusion) | data formatting | bytes 16777216 | tf_op jit(solution)/shard_map/broadcast_in_dim | solution.py:64
  928.2 97.8 %all_to_all.99 = f32[512,1,4096]{2,1,0:T(1,128)S(1)} all-to-all(f32[512,1,4096]{2,1,0:T(1,128)} %copy.84), channel_id=1, replica_groups=mesh['mode'=8,'orb'=4] {'mode'}, dimensions={0} | all-to-all | bytes 16777216 | tf_op jit(solution)/shard_map/all_to_all | solution.py:64
  1025.9 8.1 copy.134
  1034.0 8.4 copy.85
  1042.5 9.3 reshape.19
  1051.7 5.7 all-to-all-start.4
  1057.5 7.0 reduce_sum.28
  1064.6 175.6 %all-to-all-done.4 = f32[64,2,64,256]{3,2,1,0:T(8,128)} async-done(((f32[64,2,64,256]{3,2,1,0:T(8,128)}), f32[64,2,64,256]{3,2,1,0:T(8,128)}, u32[]{:S(2)}, u32[]{:S(2)}) %all-to-all-start.4) | async-done | bytes 8388640 | tf_op jit(solution)/shard_map/all_to_all | solution.py:50
  1251.1 4.5 fusion.31
  1255.6 4.0 fusion.30
  1266.8 4.1 subtract_bitcast_fusion.1
  1271.0 5.5 add_bitcast_fusion.1
  1288.7 8.0 fusion.6
  1297.6 11.5 copy.95
  1309.1 5.7 all-to-all-start.5
  1314.7 253.0 %all-to-all-done.5 = f32[16,2,256,256]{3,0,1,2:T(8,128)} async-done(((f32[16,2,256,256]{3,0,1,2:T(8,128)}), f32[16,2,256,256]{3,0,1,2:T(8,128)}, u32[]{:S(2)}, u32[]{:S(2)}) %all-to-all-start.5) | async-done | bytes 8388640 | tf_op jit(solution)/shard_map/all_to_all | solution.py:54
  1567.7 11.6 copy.96
  1579.3 6.9 reduce_sum.29
  (75 shorter events, 73.3 us)
Async XLA Ops:
  8.0 6.5 copy-start.13
  8.0 6.6 copy-start.11
  8.0 200.6 %copy-start.12 = (f32[2,64,256]{2,1,0:T(8,128)S(1)}, f32[2,64,256]{2,1,0:T(8,128)}, u32[]{:S(2)}) copy-start(f32[2,64,256]{2,1,0:T(8,128)} %param.7) | copy-start | bytes 393220
  8.0 216.6 %all-to-all-start = ((f32[64,2,64,256]{3,2,1,0:T(8,128)}), f32[64,2,64,256]{3,2,1,0:T(8,128)}, u32[]{:S(2)}, u32[]{:S(2)}) async-start(f32[64,2,64,256]{3,2,1,0:T(8,128)} %param.5), calls=%async_computation | async-start | bytes 16777216 | tf_op jit(solution)/shard_map/all_to_all | solution.py:50
  14.5 392.9 %all-gather.10.cloned.1.call-start = ((), (), s32[]{:S(2)}) async-start(), calls=%async_computation.7 | async-start | bytes 17301504 | tf_op jit(solution)/shard_map/all_gather | solution.py:43
  208.6 205.8 %copy-start.7 = (f32[2,256,256]{2,1,0:T(8,128)}, f32[2,256,256]{2,1,0:T(8,128)S(1)}, u32[]{:S(2)}) copy-start(f32[2,256,256]{2,1,0:T(8,128)S(1)} %all_gather.28) | copy-start | bytes 1572868
  224.5 189.8 %copy-start.8 = (f32[2,256,256]{2,1,0:T(8,128)}, f32[2,256,256]{2,1,0:T(8,128)S(1)}, u32[]{:S(2)}) copy-start(f32[2,256,256]{2,1,0:T(8,128)S(1)} %all_gather.27) | copy-start | bytes 1572868
  228.7 46.1 %copy-start = (f32[4,16,2,64,256]{4,3,0,1,2:T(8,128)}, f32[4,16,2,64,256]{4,3,0,1,2:T(8,128)S(1)}, u32[]{:S(2)}) copy-start(f32[4,16,2,64,256]{4,3,0,1,2:T(8,128)S(1)} %copy.64) | copy-start | bytes 25165828
  274.9 4.9 copy-start.4
  279.8 3.4 copy-start.1
  415.3 11.1 slice-start.2
  415.3 11.1 slice-start.3
  449.0 5.4 copy-start.6
  449.0 14.1 slice-start
  454.5 8.6 slice-start.1
  458.8 4.3 copy-start.5
  469.8 3.3 copy-start.2
  481.3 265.2 %all-to-all-start.1 = ((f32[16,2,256,256]{3,0,1,2:T(8,128)}), f32[16,2,256,256]{3,0,1,2:T(8,128)}, u32[]{:S(2)}, u32[]{:S(2)}) async-start(f32[16,2,256,256]{3,0,1,2:T(8,128)} %copy.81), calls=%async_computation.1 | async-start | bytes 16777216 | tf_op jit(solution)/shard_map/all_to_all | solution.py:54
  487.0 298.0 %all-gather.8.cloned.1.call-start = ((), (), s32[]{:S(2)}) async-start(), calls=%async_computation.6 | async-start | bytes 1179648 | tf_op jit(solution)/shard_map/all_gather | solution.py:63
  487.6 569.9 %all-gather.12.cloned.1.call-start = ((), (), s32[]{:S(2)}) async-start(), calls=%async_computation.8 | async-start | bytes 17301504 | tf_op jit(solution)/shard_map/all_gather | solution.py:43
  780.0 99.0 %all-to-all-start.2 = ((f32[64,8,4096]{2,0,1:T(8,128)}), f32[64,8,4096]{2,0,1:T(8,128)}, u32[]{:S(2)}, u32[]{:S(2)}) async-start(f32[64,8,4096]{2,0,1:T(8,128)} %copy.83), calls=%async_computation.2 | async-start | bytes 16777216 | tf_op jit(solution)/shard_map/all_to_all | solution.py:61
  1051.7 188.5 %all-to-all-start.4 = ((f32[64,2,64,256]{3,2,1,0:T(8,128)}), f32[64,2,64,256]{3,2,1,0:T(8,128)}, u32[]{:S(2)}, u32[]{:S(2)}) async-start(f32[64,2,64,256]{3,2,1,0:T(8,128)} %reshape.19), calls=%async_computation.4 | async-start | bytes 16777216 | tf_op jit(solution)/shard_map/all_to_all | solution.py:50
  1057.4 521.9 %all-gather.14.cloned.1.call-start = ((), (), s32[]{:S(2)}) async-start(), calls=%async_computation.9 | async-start | bytes 17301504 | tf_op jit(solution)/shard_map/all_gather | solution.py:43
  1057.5 7.0 copy-start.9
  1057.5 7.0 copy-start.10
  1285.3 3.4 copy-start.3
  1309.1 258.7 %all-to-all-start.5 = ((f32[16,2,256,256]{3,0,1,2:T(8,128)}), f32[16,2,256,256]{3,0,1,2:T(8,128)}, u32[]{:S(2)}, u32[]{:S(2)}) async-start(f32[16,2,256,256]{3,0,1,2:T(8,128)} %copy.95), calls=%async_computation.5 | async-start | bytes 16777216 | tf_op jit(solution)/shard_map/all_to_all | solution.py:54
Sparse Core Ops, SparseCore 0:
  292.0 115.4 all-gather.9
  1297.7 269.0 all-gather.13
Sparse Core Ops, SparseCore 1:
  489.4 23.6 all-gather.7
  515.9 236.7 all-gather.11
